TPU v7x, 32 devices: a whole 2x2x4 slice. The times are simulated.
32 devices in a mesh: grp: 2 (over y), scen: 4 (over z), blk: 2 (over x), sub: 2 (over core).
Axes of the slice: x: 2, y: 2, z: 4, core: 2. Of those that a mesh axis runs over, the one named last changes fastest.
Arguments:
- block_matrices: float32 [8, 256, 128, 128], P(('grp', 'scen'), ('blk', 'sub')), parts along dimension 0, may hold values from -0.25 to 0.25
- slot_row_block: int32 [8, 256], P(('grp', 'scen'), ('blk', 'sub')), parts along dimension 0, may hold values from 0 to 7
- tile_column: int32 [8, 256], P(('grp', 'scen'), ('blk', 'sub')), parts along dimension 0, may hold values from 0 to 4127, as said below
- block_count: int32 [8, 4], P(('grp', 'scen'), ('blk', 'sub')), parts along dimension 0, may hold values from 8 to 64, as said below
- carbon_scenario: int32 [8], P(('grp', 'scen')), parts along dimension 0, may hold values from 0 to 23
- intensity: float32 [24, 32, 128], P(None, ('blk', 'sub')), may hold values from 0.2 to 2
- cost_first: float32 [8192, 128], P(('grp', 'scen', 'blk', 'sub')), parts along dimension 0, may hold values from -6 to 6
- lower_first: float32 [8192, 128], P(('grp', 'scen', 'blk', 'sub')), parts along dimension 0, may hold values from -1 to -0.2
- upper_first: float32 [8192, 128], P(('grp', 'scen', 'blk', 'sub')), parts along dimension 0, may hold values from 0.2 to 1
- cost_second: float32 [8, 32, 128], P(('grp', 'scen'), ('blk', 'sub')), parts along dimension 0, may hold values from -6 to 6
- upper_second: float32 [8, 32, 128], P(('grp', 'scen'), ('blk', 'sub')), parts along dimension 0, may hold values from 0.2 to 2
- row_bound: float32 [8, 32, 128], P(('grp', 'scen'), ('blk', 'sub')), parts along dimension 0, may hold values from -20 to 20
- first_start: float32 [8192, 128], P(('grp', 'scen', 'blk', 'sub')), parts along dimension 0, may hold values from -0.2 to 0.2
- second_start: float32 [8, 32, 128], P(('grp', 'scen'), ('blk', 'sub')), parts along dimension 0, may hold values from 0 to 0.2
- dual_start: float32 [8, 32, 128], P(('grp', 'scen'), ('blk', 'sub')), parts along dimension 0, may hold values from 0 to 1
Outputs:
- first_final: float32 [8192, 128], P(('grp', 'scen', 'blk', 'sub')), parts along dimension 0
- second_final: float32 [8, 32, 128], P(('grp', 'scen'), ('blk', 'sub')), parts along dimension 0
- dual_final: float32 [8, 32, 128], P(('grp', 'scen'), ('blk', 'sub')), parts along dimension 0
- residual_norm: float32 [6], P('grp'), parts along dimension 0
There are 2 independent parts, one for each index of `grp`. A program takes and returns all parts, laid end to end along the dimension named above; an argument that names none is the same for every part. Nothing has to cross between parts.
Inputs may be any that keep to these rules, and one draw needn't show every extreme that they name: `block_count`: each scenario has one index of blk and sub with all 64 slots used; the others use between 8 and 32. `tile_column`: values below 4096 name first-section column blocks, values from 4096 on second-section ones. Split the first-section blocks into 16 equal shards in order, and take the slots of one index of scen and of blk and sub together (64 of them, scenario by scenario). In every draw, on every such device, at most 4 of them name first-section blocks of one shard, and some shard is named by exactly 4.
All inputs are finite; a program needn't handle non-finite values.
Results may differ from a plain program's by a relative error of at most 0.0003.
Values sent between devices are 32-bit elements; how exact they have to be, the bound alone decides.
No kernel may reach another device: no remote copies, remote signals or barrier semaphores. Data moves between devices by JAX's collectives and lax.ppermute only.
A program may use at most 64 MiB of HBM per device.

v0:
```python
import jax
import jax.numpy as jnp
from jax import lax
from jax.sharding import PartitionSpec as P

ITERS = 3
precise = lax.Precision.HIGHEST
step_primal = 0.4
step_dual = 0.4


def forward_window(
    block_matrices,
    onehot,
    mask,
    tile_column,
    fetch_first,
    count_first,
    second_bar,
    offset,
    window_size,
):
    count_second = second_bar.shape[1]
    is_first = tile_column < count_first
    from_first = fetch_first(tile_column, offset, window_size)
    second_index = jnp.clip(tile_column - count_first, 0, count_second - 1)
    from_second = jax.vmap(lambda table, index: table[index])(second_bar, second_index)
    blocks = jnp.where(is_first[:, :, None], from_first, from_second)
    product = jnp.einsum("skij,skj->ski", block_matrices, blocks, precision=precise)
    product = product * mask[:, :, None]
    return jnp.einsum("skr,ski->sri", onehot, product, precision=precise)


def adjoint_window(
    block_matrices,
    onehot,
    mask,
    tile_column,
    dual,
    collect_first,
    count_first,
    count_second,
    offset,
    window_size,
):
    gathered = jnp.einsum("skr,sri->ski", onehot, dual, precision=precise)
    product = jnp.einsum("skij,ski->skj", block_matrices, gathered, precision=precise)
    product = product * mask[:, :, None]
    is_first = tile_column < count_first
    first_terms = collect_first(product, tile_column, offset, window_size)
    second_index = jnp.where(is_first, count_second, tile_column - count_first)
    scenario_index = lax.broadcasted_iota(jnp.int32, second_index.shape, 0)
    second_terms = (
        jnp.zeros((product.shape[0], count_second, product.shape[2]), jnp.float32)
        .at[scenario_index, second_index]
        .add(product, mode="drop")
    )
    return (first_terms, second_terms)


def shards(
    block_matrices,
    slot_row_block,
    tile_column,
    block_count,
    carbon_scenario,
    intensity,
    cost_first,
    lower_first,
    upper_first,
    cost_second,
    upper_second,
    row_bound,
    first_start,
    second_start,
    dual_start,
):
    scen_local, slots = slot_row_block.shape
    rows_local = row_bound.shape[1]
    tile_size = row_bound.shape[2]
    shard_first = cost_first.shape[0]
    owner_count = lax.axis_size(("scen", "blk", "sub"))
    count_first = shard_first * owner_count
    count_second = cost_second.shape[1] * lax.axis_size(("blk", "sub"))
    total_cells = scen_local * rows_local * tile_size * owner_count
    mask = (jnp.arange(slots, dtype=jnp.int32)[None, :] < block_count).astype(jnp.float32)
    onehot = (
        slot_row_block[:, :, None] == jnp.arange(rows_local, dtype=jnp.int32)[None, None, :]
    ).astype(jnp.float32)
    choose = (
        carbon_scenario[:, None] == jnp.arange(intensity.shape[0], dtype=jnp.int32)[None, :]
    ).astype(jnp.float32)
    cost_total = cost_second + jnp.einsum("sc,cbt->sbt", choose, intensity, precision=precise)
    first_shape = (count_first, tile_size)

    def collect_first(product, column_window, offset, width):
        first_index = jnp.where(column_window < count_first, column_window, count_first).reshape(-1)
        return (
            jnp.zeros(first_shape, jnp.float32)
            .at[first_index]
            .add(product.reshape(-1, tile_size), mode="drop")
        )

    def make_fetch(first_source):

        def fetch_first(column_window, offset, width):
            return first_source[jnp.clip(column_window, 0, count_first - 1)]

        return fetch_first

    cost_all, lower_all, upper_all, first_now = (
        lax.all_gather(cost_first, ("scen", "blk", "sub"), axis=0, tiled=True),
        lax.all_gather(lower_first, ("scen", "blk", "sub"), axis=0, tiled=True),
        lax.all_gather(upper_first, ("scen", "blk", "sub"), axis=0, tiled=True),
        lax.all_gather(first_start, ("scen", "blk", "sub"), axis=0, tiled=True),
    )
    second_now = second_start
    dual = dual_start
    squares = []
    for step_index in range(ITERS):
        grad_first_part, grad_second_part = adjoint_window(
            block_matrices,
            onehot,
            mask,
            tile_column,
            dual,
            collect_first,
            count_first,
            count_second,
            0,
            slots,
        )
        grad_second = lax.psum_scatter(
            grad_second_part, ("blk", "sub"), scatter_dimension=1, tiled=True
        )
        grad_first = lax.psum(grad_first_part, ("scen", "blk", "sub"))
        first_next = jnp.clip(
            first_now - step_primal * (cost_all - grad_first), lower_all, upper_all
        )
        first_source = 2.0 * first_next - first_now
        second_next = jnp.clip(
            second_now - step_primal * (cost_total - grad_second), 0.0, upper_second
        )
        second_bar = lax.all_gather(
            2.0 * second_next - second_now, ("blk", "sub"), axis=1, tiled=True
        )
        residual = row_bound - forward_window(
            block_matrices,
            onehot,
            mask,
            tile_column,
            make_fetch(first_source),
            count_first,
            second_bar,
            0,
            slots,
        )
        local_square = jnp.sum(residual * residual)
        squares.append(lax.psum(local_square, ("scen", "blk", "sub")))
        dual = jnp.maximum(dual + step_dual * residual, 0.0)
        first_now = first_next
        second_now = second_next
    totals = jnp.stack(squares)
    residual_norm = jnp.sqrt(totals / total_cells)
    offset = lax.axis_index(("scen", "blk", "sub")) * shard_first
    first_final = lax.dynamic_slice_in_dim(first_now, offset, shard_first, 0)
    return (first_final, second_now, dual, residual_norm)


def solution(mesh):
    return jax.shard_map(
        shards,
        mesh=mesh,
        in_specs=(
            P(("grp", "scen"), ("blk", "sub"), None, None),
            P(("grp", "scen"), ("blk", "sub")),
            P(("grp", "scen"), ("blk", "sub")),
            P(("grp", "scen"), ("blk", "sub")),
            P(("grp", "scen")),
            P(None, ("blk", "sub"), None),
            P(("grp", "scen", "blk", "sub"), None),
            P(("grp", "scen", "blk", "sub"), None),
            P(("grp", "scen", "blk", "sub"), None),
            P(("grp", "scen"), ("blk", "sub"), None),
            P(("grp", "scen"), ("blk", "sub"), None),
            P(("grp", "scen"), ("blk", "sub"), None),
            P(("grp", "scen", "blk", "sub"), None),
            P(("grp", "scen"), ("blk", "sub"), None),
            P(("grp", "scen"), ("blk", "sub"), None),
        ),
        out_specs=(
            P(("grp", "scen", "blk", "sub"), None),
            P(("grp", "scen"), ("blk", "sub"), None),
            P(("grp", "scen"), ("blk", "sub"), None),
            P("grp"),
        ),
        check_vma=False,
    )
```

profile of v0, /device:TPU:0, one launch (start us, length us, event | category | flops | bytes accessed | tf_op | source)
XLA Modules:
  0.0 587.6 jit_solution(10443737884723280404)
XLA Ops:
  7.9 0.7 fusion.79
  8.5 0.9 fusion.66
  9.5 5.3 fusion.10
  14.8 2.3 scatter_custom_fusion
  17.2 0.7 all-gather.11.cloned.1.call-update
  17.9 0.7 all-gather.5.cloned.1.call-update
  18.7 0.5 all-gather.7.cloned.1.call-update
  19.2 0.5 all-gather.9.cloned.1.call-update
  19.9 0.9 scatter_custom_fusion.1
  21.4 0.6 dynamic-slice
  22.7 13.2 %all-reduce.1 = f32[1,32,128]{2,1,0:T(8,128)S(1)} all-reduce(f32[1,32,128]{2,1,0:T(8,128)S(1)} %bitcast.135), channel_id=2, replica_groups=mesh['grp'=2,'scen'=4,'blk'=2,'sub'=2] {'blk','sub'}, use_global_device_ids=true, to_apply=%region_3.4.clone | all-reduce | flops 4096 | bytes 32768
  36.1 5.2 all_gather.25
  41.3 0.8 gather_fusion.3
  42.1 75.8 %all-reduce.9.cloned.1.call-done = f32[4096,128]{1,0:T(8,128)} async-done(((f32[4096,128]{1,0:T(8,128)}), f32[4096,128]{1,0:T(8,128)}) %all-reduce.9.cloned.1.call-update) | async-done | bytes 2097168 | tf_op jit(solution)/shard_map/psum | solution.py:136
  117.9 43.1 %all-gather.11.cloned.1.call-done = f32[4096,128]{1,0:T(8,128)} async-done(((f32[256,128]{1,0:T(8,128)}), f32[4096,128]{1,0:T(8,128)}) %all-gather.11.cloned.1.call-update) | async-done | bytes 2097168 | tf_op jit(solution)/shard_map/all_gather | solution.py:112
  160.9 42.6 %all-gather.5.cloned.1.call-done = f32[4096,128]{1,0:T(8,128)} async-done(((f32[256,128]{1,0:T(8,128)}), f32[4096,128]{1,0:T(8,128)}) %all-gather.5.cloned.1.call-update) | async-done | bytes 2097168 | tf_op jit(solution)/shard_map/all_gather | solution.py:114
  203.6 42.5 %all-gather.7.cloned.1.call-done = f32[4096,128]{1,0:T(8,128)} async-done(((f32[256,128]{1,0:T(8,128)}), f32[4096,128]{1,0:T(8,128)}) %all-gather.7.cloned.1.call-update) | async-done | bytes 2097168 | tf_op jit(solution)/shard_map/all_gather | solution.py:113
  246.0 42.4 %all-gather.9.cloned.1.call-done = f32[4096,128]{1,0:T(8,128)} async-done(((f32[256,128]{1,0:T(8,128)}), f32[4096,128]{1,0:T(8,128)}) %all-gather.9.cloned.1.call-update) | async-done | bytes 2097168 | tf_op jit(solution)/shard_map/all_gather | solution.py:115
  288.5 5.9 %multiply_subtract_fusion.2 = (f32[4096,128]{1,0:T(8,128)S(1)}, f32[4096,128]{1,0:T(8,128)}) fusion(f32[4096,128]{1,0:T(8,128)} %all-gather.9.cloned.1.call-done, f32[4096,128]{1,0:T(8,128)} %all-gather.5.cloned.1.call-done, f32[4096,128]{1,0:T(8,128)} %all-gather.7.cloned.1.call-done, f32[4096,128]{1,0:T(8,128)} %all-gather.11.cloned.1.call-done, ...), kind=kLoop, calls=%fused_computation.28 | loop fusion | flops 3670016 | bytes 14680064 | tf_op jit(solution)/shard_map/sub | solution.py:140
  294.4 0.6 gather_fusion
  295.1 8.5 %fusion.8 = f32[64,1,128]{2,1,0:T(1,128)S(1)} fusion(f32[64,128,1]{1,2,0:T(1,128)S(1)} %bitcast.130, f32[1,64,128,128]{3,2,1,0:T(8,128)} %param.15), kind=kOutput, calls=%fused_computation.20 | convolution fusion | flops 12582912 | bytes 4259840 | tf_op jit(solution)/shard_map/skij,skj->ski/dot_general | solution.py:29
  303.6 0.3 fusion.14
  304.1 3.7 fusion.6
  307.7 2.3 scatter_custom_fusion.2
  310.1 0.9 scatter_custom_fusion.3
  311.0 10.4 %all-reduce.2 = f32[1,32,128]{2,1,0:T(8,128)S(1)} all-reduce(f32[1,32,128]{2,1,0:T(8,128)S(1)} %bitcast.137), channel_id=3, replica_groups=mesh['grp'=2,'scen'=4,'blk'=2,'sub'=2] {'blk','sub'}, use_global_device_ids=true, to_apply=%region_7.8.clone | all-reduce | flops 4096 | bytes 32768
  321.4 5.4 all_gather.26
  326.7 0.8 gather_fusion.4
  327.5 79.2 %all-reduce.11.cloned.1.call-done = f32[4096,128]{1,0:T(8,128)} async-done(((f32[4096,128]{1,0:T(8,128)}), f32[4096,128]{1,0:T(8,128)}) %all-reduce.11.cloned.1.call-update) | async-done | bytes 2097168 | tf_op jit(solution)/shard_map/psum | solution.py:136
  406.7 6.2 %multiply_subtract_fusion.1 = (f32[4096,128]{1,0:T(8,128)}, f32[4096,128]{1,0:T(8,128)}) fusion(f32[4096,128]{1,0:T(8,128)} %get-tuple-element.19, f32[4096,128]{1,0:T(8,128)} %all-gather.5.cloned.1.call-done, f32[4096,128]{1,0:T(8,128)} %all-gather.7.cloned.1.call-done, f32[4096,128]{1,0:T(8,128)S(1)} %copy-done.3, f32[4096,128]{1,0:T(8,128)} %all-reduce.11.cloned.1.call-done), kind=kLoop, calls=%fused_computation.26 | loop fusion | flops 3670016 | bytes 14680064 | tf_op jit(solution)/shard_map/sub | solution.py:140
  412.9 2.2 gather_fusion.1
  415.2 8.5 %fusion.4 = f32[64,1,128]{2,1,0:T(1,128)S(1)} fusion(f32[64,128,1]{1,2,0:T(1,128)S(1)} %bitcast.131, f32[1,64,128,128]{3,2,1,0:T(8,128)} %param.15), kind=kOutput, calls=%fused_computation.16 | convolution fusion | flops 12582912 | bytes 4259840 | tf_op jit(solution)/shard_map/skij,skj->ski/dot_general | solution.py:29
  423.6 0.3 fusion.13
  424.2 3.7 fusion.2
  427.8 2.3 scatter_custom_fusion.4
  430.2 0.9 scatter_custom_fusion.5
  431.0 10.6 %all-reduce.3 = f32[1,32,128]{2,1,0:T(8,128)S(1)} all-reduce(f32[1,32,128]{2,1,0:T(8,128)S(1)} %bitcast.136), channel_id=4, replica_groups=mesh['grp'=2,'scen'=4,'blk'=2,'sub'=2] {'blk','sub'}, use_global_device_ids=true, to_apply=%region_11.12.clone | all-reduce | flops 4096 | bytes 32768
  441.6 0.6 multiply_subtract_fusion.3
  442.2 5.4 all_gather.27
  447.6 0.8 gather_fusion.5
  448.4 79.0 %all-reduce.13.cloned.1.call-done = f32[4096,128]{1,0:T(8,128)} async-done(((f32[4096,128]{1,0:T(8,128)}), f32[4096,128]{1,0:T(8,128)}) %all-reduce.13.cloned.1.call-update) | async-done | bytes 2097168 | tf_op jit(solution)/shard_map/psum | solution.py:136
  527.3 6.2 %multiply_subtract_fusion = (f32[4096,128]{1,0:T(8,128)}, f32[4096,128]{1,0:T(8,128)}) fusion(f32[4096,128]{1,0:T(8,128)} %get-tuple-element.14, f32[4096,128]{1,0:T(8,128)} %all-gather.5.cloned.1.call-done, f32[4096,128]{1,0:T(8,128)} %all-gather.7.cloned.1.call-done, f32[4096,128]{1,0:T(8,128)S(1)} %copy-done.3, f32[4096,128]{1,0:T(8,128)} %all-reduce.13.cloned.1.call-done), kind=kLoop, calls=%fused_computation.24 | loop fusion | flops 3670016 | bytes 14680064 | tf_op jit(solution)/shard_map/sub | solution.py:140
  533.5 2.2 gather_fusion.2
  535.8 8.3 %fusion = f32[64,1,128]{2,1,0:T(1,128)S(1)} fusion(f32[64,128,1]{1,2,0:T(1,128)S(1)} %bitcast.129, f32[1,64,128,128]{3,2,1,0:T(8,128)} %param.15), kind=kOutput, calls=%fused_computation.12 | convolution fusion | flops 12582912 | bytes 4259840 | tf_op jit(solution)/shard_map/skij,skj->ski/dot_general | solution.py:29
  544.1 1.6 multiply_reduce_fusion.2
  545.7 1.6 constant_dynamic-slice_fusion
  547.2 31.1 %all-reduce.4 = (f32[1]{0:T(128)}, f32[1]{0:T(128)}, f32[1]{0:T(128)}) all-reduce(f32[1]{0:T(128)} %bitcast.54, f32[1]{0:T(128)} %bitcast.53, f32[1]{0:T(128)} %bitcast.52), channel_id=1, replica_groups=mesh['grp'=2,'scen'=4,'blk'=2,'sub'=2] {'scen','blk','sub'}, use_global_device_ids=true, to_apply=%region_17.18 | all-reduce | flops 3 | bytes 24 | tf_op jit(solution)/shard_map/psum | solution.py:159
  578.3 2.5 fusion.82
  (50 shorter events, 1.3 us)
Async XLA Ops:
  7.2 28.7 %copy-start = (f32[24,8,128]{2,1,0:T(8,128)S(1)}, f32[24,8,128]{2,1,0:T(8,128)}, u32[]{:S(2)}) copy-start(f32[24,8,128]{2,1,0:T(8,128)} %param.20) | copy-start | bytes 294916
  7.2 110.7 %all-reduce.9.cloned.1.call-start = ((), (), s32[]{:S(2)}) async-start(), calls=%async_computation.4 | async-start | bytes 4194304 | tf_op jit(solution)/shard_map/psum | solution.py:136
  14.8 5.1 copy-start.9
  14.8 6.7 %copy-start.11 = (u32[32]{0:T(128)S(1)}, u32[32]{0:T(128)}, u32[]{:S(2)}) copy-start(u32[32]{0:T(128)} %constant.109) | copy-start | bytes 388
  14.8 21.3 %copy-start.4 = (f32[1,8,128]{2,1,0:T(8,128)S(1)}, f32[1,8,128]{2,1,0:T(8,128)}, u32[]{:S(2)}) copy-start(f32[1,8,128]{2,1,0:T(8,128)} %param.25) | copy-start | bytes 12292
  14.8 21.3 %copy-start.7 = (f32[1,8,128]{2,1,0:T(8,128)S(1)}, f32[1,8,128]{2,1,0:T(8,128)}, u32[]{:S(2)}) copy-start(f32[1,8,128]{2,1,0:T(8,128)} %param.28) | copy-start | bytes 12292
  14.8 21.3 %copy-start.8 = (f32[1,8,128]{2,1,0:T(8,128)S(1)}, f32[1,8,128]{2,1,0:T(8,128)}, u32[]{:S(2)}) copy-start(f32[1,8,128]{2,1,0:T(8,128)} %param.24) | copy-start | bytes 12292
  17.1 143.8 %all-gather.11.cloned.1.call-start = ((), (), s32[]{:S(2)}) async-start(), calls=%async_computation.3 | async-start | bytes 2228224 | tf_op jit(solution)/shard_map/all_gather | solution.py:112
  17.9 185.7 %all-gather.5.cloned.1.call-start = ((), (), s32[]{:S(2)}) async-start(), calls=%async_computation | async-start | bytes 2228224 | tf_op jit(solution)/shard_map/all_gather | solution.py:114
  18.6 227.4 %all-gather.7.cloned.1.call-start = ((), (), s32[]{:S(2)}) async-start(), calls=%async_computation.1 | async-start | bytes 2228224 | tf_op jit(solution)/shard_map/all_gather | solution.py:113
  19.2 269.3 %all-gather.9.cloned.1.call-start = ((), (), s32[]{:S(2)}) async-start(), calls=%async_computation.2 | async-start | bytes 2228224 | tf_op jit(solution)/shard_map/all_gather | solution.py:115
  19.8 386.9 %all-reduce.11.cloned.1.call-start = ((), (), s32[]{:S(2)}) async-start(), calls=%async_computation.5 | async-start | bytes 4194304 | tf_op jit(solution)/shard_map/psum | solution.py:136
  295.0 8.5 %copy-start.6 = (s32[1,64]{1,0:T(1,128)S(1)}, s32[1,64]{1,0:T(1,128)}, u32[]{:S(2)}) copy-start(s32[1,64]{1,0:T(1,128)} %param.16) | copy-start | bytes 772
  295.1 8.5 %copy-start.10 = (f32[1,8,128]{2,1,0:T(8,128)S(1)}, f32[1,8,128]{2,1,0:T(8,128)}, u32[]{:S(2)}) copy-start(f32[1,8,128]{2,1,0:T(8,128)} %param.26) | copy-start | bytes 12292
  295.1 8.8 %copy-start.5 = (f32[1,8,128]{2,1,0:T(8,128)S(1)}, f32[1,8,128]{2,1,0:T(8,128)}, u32[]{:S(2)}) copy-start(f32[1,8,128]{2,1,0:T(8,128)} %param.29) | copy-start | bytes 12292
  295.1 9.0 %copy-start.1 = (f32[1,64,128,128]{3,2,1,0:T(8,128)S(1)}, f32[1,64,128,128]{3,2,1,0:T(8,128)}, u32[]{:S(2)}) copy-start(f32[1,64,128,128]{3,2,1,0:T(8,128)} %param.15) | copy-start | bytes 12582916
  307.7 99.0 %copy-start.3 = (f32[4096,128]{1,0:T(8,128)S(1)}, f32[4096,128]{1,0:T(8,128)}, u32[]{:S(2)}) copy-start(f32[4096,128]{1,0:T(8,128)} %all-gather.11.cloned.1.call-done) | copy-start | bytes 6291460
  310.0 217.3 %all-reduce.13.cloned.1.call-start = ((), (), s32[]{:S(2)}) async-start(), calls=%async_computation.6 | async-start | bytes 4194304 | tf_op jit(solution)/shard_map/psum | solution.py:136
  415.2 9.0 %copy-start.2 = (f32[1,64,128,128]{3,2,1,0:T(8,128)S(1)}, f32[1,64,128,128]{3,2,1,0:T(8,128)}, u32[]{:S(2)}) copy-start(f32[1,64,128,128]{3,2,1,0:T(8,128)} %param.15) | copy-start | bytes 12582916
Sparse Core Ops, SparseCore 0:
  17.2 100.5 all-reduce.8
  120.3 40.6 all-gather.10
  163.3 40.1 all-gather.4
  205.8 40.1 all-gather.6
  248.2 40.1 all-gather.8
  310.2 96.5 all-reduce.10
  430.3 97.0 all-reduce.12
where the time goes:
time: 588 us
  waiting for transfers between devices  407 us (69%)
  blocking collectives  81.2 us (14%)
  matrix products  41.5 us (7%)
  other arithmetic  31.8 us (5%)
  between operations  16.3 us (3%)
  local copies, waits for them, and re-layouts  9.54 us (2%)
    psum x3, waiting for transfers between devices, shards(): grad_first = lax.psum(grad_first_part, ('scen', 'blk', 'sub'))  234 us
    all_gather x1, waiting for transfers between devices, shards(): lax.all_gather(cost_first, ('scen', 'blk', 'sub'), axis=0, tiled=True)  43.1 us
    all_gather x1, waiting for transfers between devices, shards(): lax.all_gather(upper_first, ('scen', 'blk', 'sub'), axis=0, tiled=True)  42.6 us
    all_gather x1, waiting for transfers between devices, shards(): lax.all_gather(lower_first, ('scen', 'blk', 'sub'), axis=0, tiled=True)  42.5 us
    all_gather x1, waiting for transfers between devices, shards(): lax.all_gather(first_start, ('scen', 'blk', 'sub'), axis=0, tiled=True)  42.4 us
    unnamed x3, blocking collectives  34.2 us
    psum x1, blocking collectives, shards(): squares.append(lax.psum(local_square, ('scen', 'blk', 'sub')))  31.1 us
    dot_general x3, matrix products, forward_window(): jnp.einsum('skij,skj->ski', block_matrices, blocks, precision=precise)  25.2 us
  transfers between devices with their start and end apart: 7, of which 7 were waited for; matrix products, arithmetic and copies ran while one was open for 1% of the time, Pallas kernels for 0%

commit v1 on v0

--- a/solution.py
+++ b/solution.py
@@ -7,6 +7,11 @@
 precise = lax.Precision.HIGHEST
 step_primal = 0.4
 step_dual = 0.4
+
+
+def summed_here(x, mesh_axis):
+    parts = lax.all_gather(x, mesh_axis)
+    return jnp.sum(parts, axis=0)
 
 
 def forward_window(
@@ -133,7 +138,7 @@
         grad_second = lax.psum_scatter(
             grad_second_part, ("blk", "sub"), scatter_dimension=1, tiled=True
         )
-        grad_first = lax.psum(grad_first_part, ("scen", "blk", "sub"))
+        grad_first = summed_here(grad_first_part, ("scen", "blk", "sub"))
         first_next = jnp.clip(
             first_now - step_primal * (cost_all - grad_first), lower_all, upper_all
         )

time: 588 us -> 830 us (1.41)
  waiting for transfers between devices: 407 us -> 605 us
  other arithmetic: 31.8 us -> 69.9 us
    all_gather x0 -> x3, waiting for transfers between devices: none -> 444 us  [summed_here(): parts = lax.all_gather(x, mesh_axis)]
    psum x3 -> x0, waiting for transfers between devices: 234 us -> none  [shards(): grad_first = lax.psum(grad_first_part, ('scen', 'blk', 'sub'))]
    reduce_sum x0 -> x3, other arithmetic: none -> 38.1 us  [summed_here(): return jnp.sum(parts, axis=0)]
    all_gather x1, waiting for transfers between devices: 42.6 us -> 32.1 us  [shards(): lax.all_gather(upper_first, ('scen', 'blk', 'sub'), axis=0, tiled=True)]
  transfers between devices with their start and end apart: 7 -> 7, of which waited for: 7 -> 7; matrix products, arithmetic and copies ran while one was open for 1% -> 2% of each run, Pallas kernels for 0% -> 0%
where the time goes in v1:
time: 830 us
  waiting for transfers between devices  605 us (73%)
  blocking collectives  85 us (10%)
  other arithmetic  69.9 us (8%)
  matrix products  41.8 us (5%)
  between operations  16.4 us (2%)
  local copies, waits for them, and re-layouts  11.1 us (1%)
    all_gather x3, waiting for transfers between devices, summed_here(): parts = lax.all_gather(x, mesh_axis)  444 us
    all_gather x1, waiting for transfers between devices, shards(): lax.all_gather(lower_first, ('scen', 'blk', 'sub'), axis=0, tiled=True)  42.4 us
    all_gather x1, waiting for transfers between devices, shards(): lax.all_gather(cost_first, ('scen', 'blk', 'sub'), axis=0, tiled=True)  42.2 us
    all_gather x1, waiting for transfers between devices, shards(): lax.all_gather(first_start, ('scen', 'blk', 'sub'), axis=0, tiled=True)  42.2 us
    reduce_sum x3, other arithmetic, summed_here(): return jnp.sum(parts, axis=0)  38.1 us
    unnamed x3, blocking collectives  35.8 us
    psum x1, blocking collectives, shards(): squares.append(lax.psum(local_square, ('scen', 'blk', 'sub')))  33.4 us
    all_gather x1, waiting for transfers between devices, shards(): lax.all_gather(upper_first, ('scen', 'blk', 'sub'), axis=0, tiled=True)  32.1 us
  transfers between devices with their start and end apart: 7, of which 7 were waited for; matrix products, arithmetic and copies ran while one was open for 2% of the time, Pallas kernels for 0%

profile of v1, /device:TPU:0, one launch (start us, length us, event | category | flops | bytes accessed | tf_op | source)
XLA Modules:
  0.0 829.7 jit_solution(3357280426610749607)
XLA Ops:
  7.9 0.7 fusion.79
  8.5 0.9 fusion.66
  9.5 5.3 fusion.10
  14.8 2.3 scatter_custom_fusion
  17.1 0.7 all-gather.11.cloned.1.call-update
  17.9 0.7 all-gather.13.cloned.1.call-update
  19.2 0.5 all-gather.15.cloned.1.call-update
  19.8 0.9 scatter_custom_fusion.1
  21.4 0.6 dynamic-slice
  22.6 13.4 %all-reduce.1 = f32[1,32,128]{2,1,0:T(8,128)S(1)} all-reduce(f32[1,32,128]{2,1,0:T(8,128)S(1)} %bitcast.141), channel_id=5, replica_groups=mesh['grp'=2,'scen'=4,'blk'=2,'sub'=2] {'blk','sub'}, use_global_device_ids=true, to_apply=%region_3.4.clone | all-reduce | flops 4096 | bytes 32768
  36.2 5.2 all_gather.45
  41.4 0.8 gather_fusion.3
  42.3 145.7 %all-gather.19.cloned.1.call-done = f32[65536,128]{1,0:T(8,128)} async-done(((f32[4096,128]{1,0:T(8,128)}), f32[65536,128]{1,0:T(8,128)}) %all-gather.19.cloned.1.call-update) | async-done | bytes 33554448 | tf_op jit(solution)/shard_map/all_gather | solution.py:13
  188.0 11.8 %reduce_sum.54 = f32[4096,128]{1,0:T(8,128)S(1)} reduce(f32[16,4096,128]{2,1,0:T(8,128)} %bitcast.126, f32[]{:T(128)} %constant.16.clone.1), dimensions={0}, to_apply=%region_1.2 | reduce | flops 7864320 | bytes 35651588 | tf_op jit(solution)/shard_map/reduce_sum | solution.py:14
  199.8 32.1 %all-gather.11.cloned.1.call-done = f32[4096,128]{1,0:T(8,128)} async-done(((f32[256,128]{1,0:T(8,128)}), f32[4096,128]{1,0:T(8,128)}) %all-gather.11.cloned.1.call-update) | async-done | bytes 2097168 | tf_op jit(solution)/shard_map/all_gather | solution.py:119
  232.0 42.4 %all-gather.13.cloned.1.call-done = f32[4096,128]{1,0:T(8,128)} async-done(((f32[256,128]{1,0:T(8,128)}), f32[4096,128]{1,0:T(8,128)}) %all-gather.13.cloned.1.call-update) | async-done | bytes 2097168 | tf_op jit(solution)/shard_map/all_gather | solution.py:118
  274.3 42.2 %all-gather.17.cloned.1.call-done = f32[4096,128]{1,0:T(8,128)} async-done(((f32[256,128]{1,0:T(8,128)}), f32[4096,128]{1,0:T(8,128)}) %all-gather.17.cloned.1.call-update) | async-done | bytes 2097168 | tf_op jit(solution)/shard_map/all_gather | solution.py:117
  316.6 42.2 %all-gather.15.cloned.1.call-done = f32[4096,128]{1,0:T(8,128)} async-done(((f32[256,128]{1,0:T(8,128)}), f32[4096,128]{1,0:T(8,128)}) %all-gather.15.cloned.1.call-update) | async-done | bytes 2097168 | tf_op jit(solution)/shard_map/all_gather | solution.py:120
  358.8 6.0 multiply_subtract_fusion.2
  364.8 2.2 gather_fusion
  367.1 8.6 %fusion.8 = f32[64,1,128]{2,1,0:T(1,128)S(1)} fusion(f32[64,128,1]{1,2,0:T(1,128)S(1)} %bitcast.136, f32[1,64,128,128]{3,2,1,0:T(8,128)} %param.15), kind=kOutput, calls=%fused_computation.20 | convolution fusion | flops 12582912 | bytes 4259840 | tf_op jit(solution)/shard_map/skij,skj->ski/dot_general | solution.py:34
  376.3 3.7 fusion.6
  379.9 2.3 scatter_custom_fusion.2
  382.3 1.1 scatter_custom_fusion.3
  383.4 10.9 %all-reduce.2 = f32[1,32,128]{2,1,0:T(8,128)S(1)} all-reduce(f32[1,32,128]{2,1,0:T(8,128)S(1)} %bitcast.143), channel_id=6, replica_groups=mesh['grp'=2,'scen'=4,'blk'=2,'sub'=2] {'blk','sub'}, use_global_device_ids=true, to_apply=%region_7.8.clone | all-reduce | flops 4096 | bytes 32768
  394.3 5.2 all_gather.48
  399.5 0.8 gather_fusion.4
  400.3 148.9 %all-gather.21.cloned.1.call-done = f32[65536,128]{1,0:T(8,128)} async-done(((f32[4096,128]{1,0:T(8,128)}), f32[65536,128]{1,0:T(8,128)}) %all-gather.21.cloned.1.call-update) | async-done | bytes 33554448 | tf_op jit(solution)/shard_map/all_gather | solution.py:13
  549.3 13.3 %reduce_sum.55 = f32[4096,128]{1,0:T(8,128)} reduce(f32[16,4096,128]{2,1,0:T(8,128)} %bitcast.128, f32[]{:T(128)} %constant.16.clone.1), dimensions={0}, to_apply=%region_5.6 | reduce | flops 7864320 | bytes 35651588 | tf_op jit(solution)/shard_map/reduce_sum | solution.py:14
  562.5 6.1 multiply_subtract_fusion.1
  568.6 2.2 gather_fusion.1
  570.9 8.6 %fusion.4 = f32[64,1,128]{2,1,0:T(1,128)S(1)} fusion(f32[64,128,1]{1,2,0:T(1,128)S(1)} %bitcast.137, f32[1,64,128,128]{3,2,1,0:T(8,128)} %param.15), kind=kOutput, calls=%fused_computation.16 | convolution fusion | flops 12582912 | bytes 4259840 | tf_op jit(solution)/shard_map/skij,skj->ski/dot_general | solution.py:34
  580.0 3.7 fusion.2
  583.7 2.3 scatter_custom_fusion.4
  586.0 0.9 scatter_custom_fusion.5
  586.8 11.5 %all-reduce.3 = f32[1,32,128]{2,1,0:T(8,128)S(1)} all-reduce(f32[1,32,128]{2,1,0:T(8,128)S(1)} %bitcast.142), channel_id=7, replica_groups=mesh['grp'=2,'scen'=4,'blk'=2,'sub'=2] {'blk','sub'}, use_global_device_ids=true, to_apply=%region_11.12.clone | all-reduce | flops 4096 | bytes 32768
  598.3 0.6 multiply_subtract_fusion.3
  598.9 5.4 all_gather.51
  604.4 0.8 gather_fusion.5
  605.2 149.2 %all-gather.23.cloned.1.call-done = f32[65536,128]{1,0:T(8,128)} async-done(((f32[4096,128]{1,0:T(8,128)}), f32[65536,128]{1,0:T(8,128)}) %all-gather.23.cloned.1.call-update) | async-done | bytes 33554448 | tf_op jit(solution)/shard_map/all_gather | solution.py:13
  754.3 13.0 %reduce_sum.56 = f32[4096,128]{1,0:T(8,128)} reduce(f32[16,4096,128]{2,1,0:T(8,128)} %bitcast.127, f32[]{:T(128)} %constant.16.clone.1), dimensions={0}, to_apply=%region_9.10 | reduce | flops 7864320 | bytes 35651588 | tf_op jit(solution)/shard_map/reduce_sum | solution.py:14
  767.4 6.0 multiply_subtract_fusion
  773.3 2.2 gather_fusion.2
  775.6 8.3 %fusion = f32[64,1,128]{2,1,0:T(1,128)S(1)} fusion(f32[64,128,1]{1,2,0:T(1,128)S(1)} %bitcast.135, f32[1,64,128,128]{3,2,1,0:T(8,128)} %param.15), kind=kOutput, calls=%fused_computation.12 | convolution fusion | flops 12582912 | bytes 4259840 | tf_op jit(solution)/shard_map/skij,skj->ski/dot_general | solution.py:34
  784.0 1.5 multiply_reduce_fusion.2
  785.5 1.6 constant_dynamic-slice_fusion
  787.0 33.4 %all-reduce.4 = (f32[1]{0:T(128)}, f32[1]{0:T(128)}, f32[1]{0:T(128)}) all-reduce(f32[1]{0:T(128)} %bitcast.57, f32[1]{0:T(128)} %bitcast.56, f32[1]{0:T(128)} %bitcast.55), channel_id=1, replica_groups=mesh['grp'=2,'scen'=4,'blk'=2,'sub'=2] {'scen','blk','sub'}, use_global_device_ids=true, to_apply=%region_17.18 | all-reduce | flops 3 | bytes 24 | tf_op jit(solution)/shard_map/psum | solution.py:164
  820.4 2.5 fusion.82
  (55 shorter events, 2.4 us)
Async XLA Ops:
  7.2 28.8 %copy-start = (f32[24,8,128]{2,1,0:T(8,128)S(1)}, f32[24,8,128]{2,1,0:T(8,128)}, u32[]{:S(2)}) copy-start(f32[24,8,128]{2,1,0:T(8,128)} %param.20) | copy-start | bytes 294916
  7.2 180.8 %all-gather.19.cloned.1.call-start = ((), (), s32[]{:S(2)}) async-start(), calls=%async_computation.4 | async-start | bytes 35651584 | tf_op jit(solution)/shard_map/all_gather | solution.py:13
  14.8 5.0 copy-start.10
  14.8 6.6 copy-start.12
  14.8 21.4 %copy-start.5 = (f32[1,8,128]{2,1,0:T(8,128)S(1)}, f32[1,8,128]{2,1,0:T(8,128)}, u32[]{:S(2)}) copy-start(f32[1,8,128]{2,1,0:T(8,128)} %param.25) | copy-start | bytes 12292
  14.8 21.4 %copy-start.8 = (f32[1,8,128]{2,1,0:T(8,128)S(1)}, f32[1,8,128]{2,1,0:T(8,128)}, u32[]{:S(2)}) copy-start(f32[1,8,128]{2,1,0:T(8,128)} %param.28) | copy-start | bytes 12292
  14.8 21.4 %copy-start.9 = (f32[1,8,128]{2,1,0:T(8,128)S(1)}, f32[1,8,128]{2,1,0:T(8,128)}, u32[]{:S(2)}) copy-start(f32[1,8,128]{2,1,0:T(8,128)} %param.24) | copy-start | bytes 12292
  17.1 214.9 %all-gather.11.cloned.1.call-start = ((), (), s32[]{:S(2)}) async-start(), calls=%async_computation | async-start | bytes 2228224 | tf_op jit(solution)/shard_map/all_gather | solution.py:119
  17.8 256.5 %all-gather.13.cloned.1.call-start = ((), (), s32[]{:S(2)}) async-start(), calls=%async_computation.1 | async-start | bytes 2228224 | tf_op jit(solution)/shard_map/all_gather | solution.py:118
  18.6 298.0 %all-gather.17.cloned.1.call-start = ((), (), s32[]{:S(2)}) async-start(), calls=%async_computation.3 | async-start | bytes 2228224 | tf_op jit(solution)/shard_map/all_gather | solution.py:117
  19.1 339.6 %all-gather.15.cloned.1.call-start = ((), (), s32[]{:S(2)}) async-start(), calls=%async_computation.2 | async-start | bytes 2228224 | tf_op jit(solution)/shard_map/all_gather | solution.py:120
  19.7 529.5 %all-gather.21.cloned.1.call-start = ((), (), s32[]{:S(2)}) async-start(), calls=%async_computation.5 | async-start | bytes 35651584 | tf_op jit(solution)/shard_map/all_gather | solution.py:13
  367.1 8.7 %copy-start.7 = (s32[1,64]{1,0:T(1,128)S(1)}, s32[1,64]{1,0:T(1,128)}, u32[]{:S(2)}) copy-start(s32[1,64]{1,0:T(1,128)} %param.16) | copy-start | bytes 772
  367.1 8.7 %copy-start.11 = (f32[1,8,128]{2,1,0:T(8,128)S(1)}, f32[1,8,128]{2,1,0:T(8,128)}, u32[]{:S(2)}) copy-start(f32[1,8,128]{2,1,0:T(8,128)} %param.26) | copy-start | bytes 12292
  367.1 8.9 %copy-start.6 = (f32[1,8,128]{2,1,0:T(8,128)S(1)}, f32[1,8,128]{2,1,0:T(8,128)}, u32[]{:S(2)}) copy-start(f32[1,8,128]{2,1,0:T(8,128)} %param.29) | copy-start | bytes 12292
  367.1 9.1 %copy-start.2 = (f32[1,64,128,128]{3,2,1,0:T(8,128)S(1)}, f32[1,64,128,128]{3,2,1,0:T(8,128)}, u32[]{:S(2)}) copy-start(f32[1,64,128,128]{3,2,1,0:T(8,128)} %param.15) | copy-start | bytes 12582916
  382.3 372.1 %all-gather.23.cloned.1.call-start = ((), (), s32[]{:S(2)}) async-start(), calls=%async_computation.6 | async-start | bytes 35651584 | tf_op jit(solution)/shard_map/all_gather | solution.py:13
  549.3 13.3 %copy-start.4 = (f32[4096,128]{1,0:T(8,128)S(1)}, f32[4096,128]{1,0:T(8,128)}, u32[]{:S(2)}) copy-start(f32[4096,128]{1,0:T(8,128)} %all-gather.11.cloned.1.call-done) | copy-start | bytes 6291460
  570.9 9.1 %copy-start.3 = (f32[1,64,128,128]{3,2,1,0:T(8,128)S(1)}, f32[1,64,128,128]{3,2,1,0:T(8,128)}, u32[]{:S(2)}) copy-start(f32[1,64,128,128]{3,2,1,0:T(8,128)} %param.15) | copy-start | bytes 12582916
  775.6 47.3 %copy-start.1 = (f32[24,8,128]{2,1,0:T(8,128)S(1)}, f32[24,8,128]{2,1,0:T(8,128)}, u32[]{:S(2)}) copy-start(f32[24,8,128]{2,1,0:T(8,128)} %param.20) | copy-start | bytes 294916
Sparse Core Ops, SparseCore 0:
  17.2 170.7 all-gather.18
  190.2 41.7 all-gather.10
  234.1 40.1 all-gather.12
  276.4 40.1 all-gather.16
  318.6 40.1 all-gather.14
  382.4 166.8 all-gather.20
  586.1 168.2 all-gather.22
